TPU v7x, 256 devices: a whole 4x4x8 slice. The times are simulated.
256 devices in a mesh: row: 16 (over z_lo, x), col: 16 (over z_hi, y, core).
Axes of the slice: x: 4, y: 4, z: 8 (z_hi: 2, z_lo: 4; z = z_hi * 4 + z_lo), core: 2. Of those that a mesh axis runs over, the one named last changes fastest.
Arguments:
- amplitudes: bfloat16 [65536, 768], P(('row', 'col')), may hold values from -6 to 6
- integrals: bfloat16 [65536, 768], P(('row', 'col')), may hold values from -0.21875 to 0.21875
- block_mask: int32 [512, 512], P('row'), may hold values from 0 to 1, as said below
- occ_energy: float32 [64], replicated, may hold values from -1.5 to -0.5
- vir_energy: float32 [1024], replicated, may hold values from 0.1 to 1.5
Outputs:
- update: bfloat16 [16, 16, 192, 128, 128], P('row', 'col')
Inputs may be any that keep to these rules, and one draw needn't show every extreme that they name: block_mask is symmetric; among the 2 x 2 blocks (a, b) with the same a // 2 and b // 2 at most one is present, and for every a // 2 one block with b // 2 = a // 2 and b = a is present; for every cell (r, c) at most 192 of its blocks are present, with exactly 192 in some cell.
All inputs are finite; a program needn't handle non-finite values.
Results may differ from a plain program's by a relative error of at most 0.0049.
Values may be sent and summed in bfloat16 or wider, within the bound.
A program may use at most 64 MiB of HBM per device.

v0:
```python
import jax
import jax.numpy as jnp
from jax import lax
from jax.sharding import PartitionSpec as P

BLOCK = 128
SHARD_BLOCKS = 2
TILES = 192


def slot_layout(rows_mask, col_at, nrow, ncol, split, limit):
    tile_mask = lax.dynamic_index_in_dim(
        rows_mask.reshape(ncol * split, nrow, ncol, split), col_at, 2, keepdims=False
    )
    flat = tile_mask.reshape(-1)
    wide = nrow * split
    cells = ncol * split * wide
    places = jnp.arange(cells, dtype=jnp.int32)
    keys = jnp.where(flat > 0, places, places + cells)
    picked = jnp.argsort(keys, stable=True)[:limit]
    present = flat[picked] > 0
    return (picked // wide, picked % wide, present)


def block_products(left, left_pick, right, right_pick):
    groups = left_pick.shape[0] // 8

    def one_group(picks):
        left_rows, right_rows = picks
        return jnp.einsum(
            "sik,sjk->sij", left[left_rows], right[right_rows], preferred_element_type=jnp.float32
        ).astype(jnp.bfloat16)

    result = lax.map(one_group, (left_pick.reshape(groups, 8), right_pick.reshape(groups, 8)))
    return result.reshape(left_pick.shape[0], left.shape[1], right.shape[1])


def shards(amplitudes, integrals, block_mask, occ_energy, vir_energy):
    nrow = lax.axis_size("row")
    ncol = lax.axis_size("col")
    split = SHARD_BLOCKS
    block = BLOCK
    cells = nrow * ncol
    limit = min(TILES, cells)
    row_at = lax.axis_index("row")
    col_at = lax.axis_index("col")
    width = amplitudes.shape[1]
    upick, vpick, present = slot_layout(block_mask, col_at, nrow, ncol, split, limit)
    row_block = row_at * ncol * split + upick
    col_block = (vpick // split * ncol + col_at) * split + vpick % split
    gaps = (vir_energy[None, :] - occ_energy[:, None]).reshape(cells * split, block)
    denom = (
        jnp.take(gaps, row_block, axis=0)[:, :, None]
        + jnp.take(gaps, col_block, axis=0)[:, None, :]
    )
    amp_here = lax.all_gather(amplitudes, "col", axis=0, tiled=True)
    int_there = lax.all_gather(integrals, "row", axis=0, tiled=True)
    direct = block_products(
        amp_here.reshape(ncol * split, block, width),
        upick,
        int_there.reshape(nrow * split, block, width),
        vpick,
    )
    kept = jnp.where(present[:, None, None], direct, jnp.zeros_like(direct))
    group_u = upick // split
    group_v = vpick // split
    layout = (
        jnp.zeros((ncol, nrow, 1, block, block), jnp.bfloat16).at[group_u, group_v, 0].add(kept)
    )
    moved = lax.all_to_all(
        lax.all_to_all(layout, "row", split_axis=1, concat_axis=2, tiled=True),
        "col",
        split_axis=0,
        concat_axis=1,
        tiled=True,
    )
    mirror = jnp.swapaxes(moved[0][group_u, group_v], 1, 2)
    total = (direct.astype(jnp.float32) + mirror.astype(jnp.float32)) / denom
    update = jnp.where(present[:, None, None], total, jnp.float32(0.0)).astype(jnp.bfloat16)
    return update.reshape(1, 1, limit, block, block)


def solution(mesh):
    in_specs = (P(("row", "col"), None), P(("row", "col"), None), P("row", None), P(), P())
    out_specs = P("row", "col", None, None, None)
    return jax.shard_map(shards, mesh=mesh, in_specs=in_specs, out_specs=out_specs, check_vma=False)
```

profile of v0, /device:TPU:89, one launch (start us, length us, event | category | flops | bytes accessed | tf_op | source)
XLA Modules:
  0.0 924.2 jit_solution(3538350199110569554)
XLA Ops:
  9.4 4.4 sort.17
  15.2 87.1 %all-gather.3.cloned.1.call-done = bf16[4096,768]{1,0:T(8,128)(2,1)} async-done(((bf16[256,768]{1,0:T(8,128)(2,1)}), bf16[4096,768]{1,0:T(8,128)(2,1)}) %all-gather.3.cloned.1.call-update) | async-done | bytes 6291472 | tf_op jit(solution)/shard_map/all_gather | solution.py:56
  102.3 74.7 %all-gather.5.cloned.1.call-done = bf16[4096,768]{1,0:T(8,128)(2,1)} async-done(((bf16[256,768]{1,0:T(8,128)(2,1)}), bf16[4096,768]{1,0:T(8,128)(2,1)}) %all-gather.5.cloned.1.call-update) | async-done | bytes 6291472 | tf_op jit(solution)/shard_map/all_gather | solution.py:57
  177.0 201.6 %while.10 = (s32[]{:T(128)}, bf16[24,8,128,128]{2,3,1,0:T(8,128)(2,1)}, s32[24,8]{1,0:T(8,128)S(1)}, bf16[32,128,768]{2,1,0:T(8,128)(2,1)}, s32[24,8]{1,0:T(8,12...) while((s32[]{:T(128)}, bf16[24,8,128,128]{2,3,1,0:T(8,128)(2,1)}, s32[24,8]{1,0:T(8,128)S(1)}, ...), condition=%wide.region_2.3_spmd, body=%wide.region_1.2_spmd.sunk | while | flops 201459760 | bytes 10756945 | solution.py:34
  177.0 3.4 gather_fusion
  180.4 3.4 gather_fusion.1
  185.4 3.4 gather_fusion
  188.8 3.4 gather_fusion.1
  193.8 3.4 gather_fusion
  197.2 3.4 gather_fusion.1
  202.2 3.4 gather_fusion
  205.6 3.4 gather_fusion.1
  210.6 3.4 gather_fusion
  214.0 3.4 gather_fusion.1
  219.0 3.4 gather_fusion
  222.4 3.4 gather_fusion.1
  227.4 3.4 gather_fusion
  230.8 3.4 gather_fusion.1
  235.8 3.4 gather_fusion
  239.2 3.4 gather_fusion.1
  247.6 3.4 gather_fusion.1
  252.6 3.4 gather_fusion
  264.4 3.4 gather_fusion.1
  269.4 3.4 gather_fusion
  281.2 3.4 gather_fusion.1
  286.2 3.4 gather_fusion
  298.0 3.4 gather_fusion.1
  303.0 3.4 gather_fusion
  314.8 3.4 gather_fusion.1
  319.8 3.4 gather_fusion
  331.6 3.4 gather_fusion.1
  336.6 3.4 gather_fusion
  348.4 3.4 gather_fusion.1
  353.4 3.4 gather_fusion
  365.2 3.4 gather_fusion.1
  370.2 3.4 gather_fusion
  378.6 5.9 bitcast_select_fusion
  384.5 8.6 copy.18
  393.1 5.4 broadcast.125
  398.4 39.9 %scatter_fusion = bf16[16,16,128,128]{3,2,1,0:T(8,128)(2,1)} fusion(bf16[16,16,128,128]{3,2,1,0:T(8,128)(2,1)} %broadcast.125, s32[192]{0:T(256)S(1)} %bitcast.63, bf16[192,128,128]{2,1,0:T(8,128)(2,1)} %copy.18), kind=kCustom, calls=%fused_computation.6 | custom fusion | flops 3145728 | bytes 18875904 | tf_op jit(solution)/shard_map/scatter-add | solution.py:68
  438.3 10.3 %copy.19 = bf16[16,16,1,128,128]{4,3,0,2,1:T(8,128)(2,1)} copy(bf16[16,16,1,128,128]{4,3,1,0,2:T(8,128)(2,1)} %bitcast.58) | data formatting | bytes 16777216 | tf_op jit(solution)/shard_map/scatter-add | solution.py:68
  448.6 194.4 %all_to_all.21 = bf16[16,16,1,128,128]{4,3,0,2,1:T(8,128)(2,1)} all-to-all(bf16[16,16,1,128,128]{4,3,0,2,1:T(8,128)(2,1)} %copy.19), channel_id=1, replica_groups=mesh['row'=16,'col'=16] {'row'}, dimensions={1} | all-to-all | bytes 16777216 | tf_op jit(solution)/shard_map/all_to_all | solution.py:71
  643.0 10.3 %copy.20 = bf16[16,1,16,128,128]{4,3,2,1,0:T(8,128)(2,1)} copy(bf16[16,1,16,128,128]{4,3,0,2,1:T(8,128)(2,1)} %bitcast.59) | data formatting | bytes 16777216 | tf_op jit(solution)/shard_map/all_to_all | solution.py:71
  653.4 11.0 %all-to-all-start.1 = ((bf16[16,1,16,128,128]{4,3,2,1,0:T(8,128)(2,1)}), bf16[16,1,16,128,128]{4,3,2,1,0:T(8,128)(2,1)}, u32[]{:S(2)}, u32[]{:S(2)}) async-start(bf16[16,1,16,128,128]{4,3,2,1,0:T(8,128)(2,1)} %copy.20), calls=%async_computation.1 | async-start | bytes 16777216 | tf_op jit(solution)/shard_map/all_to_all | solution.py:70
  666.2 220.9 %all-to-all-done.1 = bf16[16,1,16,128,128]{4,3,2,1,0:T(8,128)(2,1)} async-done(((bf16[16,1,16,128,128]{4,3,2,1,0:T(8,128)(2,1)}), bf16[16,1,16,128,128]{4,3,2,1,0:T(8,128)(2,1)}, u32[]{:S(2)}, u32[]{:S(2)}) %all-to-all-start.1) | async-done | bytes 8388640 | tf_op jit(solution)/shard_map/all_to_all | solution.py:70
  887.1 12.8 %gather_fusion.3 = bf16[192,128,128]{2,1,0:T(8,128)(2,1)} fusion(bf16[16,16,128,128]{3,2,1,0:T(8,128)(2,1)} %bitcast.14, s32[192]{0:T(256)S(1)} %get-tuple-element.59), kind=kCustom, calls=%fused_computation.5 | custom fusion | bytes 12584448 | tf_op jit(solution)/shard_map/gather | solution.py:77
  899.9 8.8 fusion.7
  908.7 8.6 copy.21
  (193 shorter events, 96.9 us)
Async XLA Ops:
  6.5 95.7 %all-gather.3.cloned.1.call-start = ((), (), s32[]{:S(2)}) async-start(), calls=%async_computation.2 | async-start | bytes 6684672 | tf_op jit(solution)/shard_map/all_gather | solution.py:56
  7.3 169.7 %all-gather.5.cloned.1.call-start = ((), (), s32[]{:S(2)}) async-start(), calls=%async_computation.3 | async-start | bytes 6684672 | tf_op jit(solution)/shard_map/all_gather | solution.py:57
  653.4 11.0 %copy-start.1 = (f32[64]{0:T(128)S(1)}, f32[64]{0:T(128)}, u32[]{:S(2)}) copy-start(f32[64]{0:T(128)} %param.12) | copy-start | bytes 772
  653.4 11.1 %copy-start = (f32[1024]{0:T(1024)S(1)}, f32[1024]{0:T(1024)}, u32[]{:S(2)}) copy-start(f32[1024]{0:T(1024)} %param.13) | copy-start | bytes 12292
  653.4 233.7 %all-to-all-start.1 = ((bf16[16,1,16,128,128]{4,3,2,1,0:T(8,128)(2,1)}), bf16[16,1,16,128,128]{4,3,2,1,0:T(8,128)(2,1)}, u32[]{:S(2)}, u32[]{:S(2)}) async-start(bf16[16,1,16,128,128]{4,3,2,1,0:T(8,128)(2,1)} %copy.20), calls=%async_computation.1 | async-start | bytes 16777216 | tf_op jit(solution)/shard_map/all_to_all | solution.py:70
Sparse Core Ops, SparseCore 0:
  10.1 92.1 all-gather.2
  104.1 72.8 all-gather.4
where the time goes:
time: 927 us; the launch traced here: 924 us
  waiting for transfers between devices  384 us (41%)
  local copies, waits for them, and re-layouts  247 us (27%)
  blocking collectives  194 us (21%)
  other arithmetic  59.9 us (6%)
  matrix products  13.7 us (1%)
  between operations  13.6 us (1%)
  starting transfers between devices  11 us (1%)
    all_to_all x1, waiting for transfers between devices, shards(): lax.all_to_all(lax.all_to_all(layout, 'row', split_axis=1, concat_axis=2,...  221 us
    all_to_all x1, blocking collectives, shards(): lax.all_to_all(layout, 'row', split_axis=1, concat_axis=2, tiled=True)  194 us
    all_gather x1, waiting for transfers between devices, shards(): amp_here = lax.all_gather(amplitudes, 'col', axis=0, tiled=True)  87.1 us
    gather x24, local copies, waits for them, and re-layouts, one_group(): left[left_rows]  82.4 us
    gather x24, local copies, waits for them, and re-layouts, one_group(): right[right_rows]  82.4 us
    all_gather x1, waiting for transfers between devices, shards(): int_there = lax.all_gather(integrals, 'row', axis=0, tiled=True)  74.7 us
    scatter-add x1, other arithmetic, shards(): jnp.zeros((ncol, nrow, 1, block, block), jnp.bfloat16)  39.9 us
    dynamic_update_slice x48, local copies, waits for them, and re-layouts, block_products(): lax.map(one_group, (left_pick.reshape(groups, 8), right_pick.reshape(grou...  21.7 us
  transfers between devices with their start and end apart: 3, of which 3 were waited for; matrix products, arithmetic and copies ran while one was open for 1% of the time, Pallas kernels for 0%

commit v1 on v0

v1 whole, which is shorter than its diff:
```python
import functools

import jax
import jax.numpy as jnp
from jax import lax
from jax.experimental import pallas as pl
from jax.experimental.pallas import tpu as pltpu
from jax.sharding import PartitionSpec as P

BLOCK = 128
UNIT = 256
DEPTH = 768
TILES = 192
GRID = 16
CELLS = GRID * GRID
MESH = pl.DeviceIdType.MESH

OWN = 6
CROSS = 7
UNITS = 19


def table(at, values):
    out = jnp.int32(values[0])
    for i in range(1, len(values)):
        out = jnp.where(at == i, jnp.int32(values[i]), out)
    return out


def names():
    keys = []
    for flow in (0, 1):
        for dist in (1, 2, 3):
            for piece in (0, 1):
                keys.append(("z", flow, dist, piece))
        keys.append(("z", flow, 4, flow))
    for k in range(4):
        for flow in (0, 1):
            for piece in (0, 1):
                keys.append(("x", k, flow, piece))
            keys.append(("xf", k, flow))
    for h in (0, 1):
        for flow in (0, 1):
            for piece in (0, 1):
                keys.append(("y", h, flow, piece))
            keys.append(("yf", h, flow))
        for dy in range(4):
            for piece in (0, 1):
                keys.append(("c", h, dy, piece))
    return {key: i for i, key in enumerate(keys)}


KEYS = names()


def exchange(pick, amp, ints, side_of, grow, gcol, dense, store, near, far, gaps, stage, local_sem, send_sem, recv_sem, out_sem):
    row, col = lax.axis_index("row"), lax.axis_index("col")
    zl, x = row // 4, row % 4
    zh, y, core = col // 8, (col // 2) % 4, col % 2
    z = zh * 4 + zl

    def at_x(step):
        return (zl * 4 + (x + step) % 4, col)

    def at_y(step):
        return (row, zh * 8 + ((y + step) % 4) * 2 + core)

    def at_z(step):
        there = (z + step) % 8
        return ((there % 4) * 4 + x, (there // 4) * 8 + y * 2 + core)

    partner = (row, zh * 8 + y * 2 + (1 - core))
    step_of = (1, 3)
    ring_of = (1, 7)

    own_copies = []
    for piece, src in enumerate((amp, ints)):
        own_copies.append(pltpu.make_async_copy(src, near.at[0, piece], local_sem.at[piece]))
        own_copies.append(pltpu.make_async_copy(src, store.at[OWN, piece], local_sem.at[2 + piece]))
    for copy in own_copies:
        copy.start()

    barrier = pltpu.get_barrier_semaphore()
    for there in (at_x(1), at_x(3), at_y(1), at_y(3), at_z(1), at_z(7), partner):
        pl.semaphore_signal(barrier, inc=1, device_id=there, device_id_type=MESH)
    pl.semaphore_wait(barrier, 7)
    for copy in own_copies:
        copy.wait()

    slot_k = [OWN] + [table(zl, v) for v in ((3, 0, 3, 0), (4, 3, 0, 1), (5, 4, 1, 2))]
    line_k = [zl] + [table(zl, v) for v in ((1, 0, 3, 2), (2, 2, 1, 1), (3, 3, 0, 0))]

    started = []

    def descriptor(key):
        i = KEYS[key]
        kind = key[0]
        if kind == "z":
            _, flow, dist, piece = key
            src = near.at[0, piece] if dist == 1 else store.at[flow * 3 + dist - 2, piece]
            dst = far.at[0, piece] if dist == 4 else store.at[flow * 3 + dist - 1, piece]
            there = at_z(ring_of[flow])
        elif kind == "x":
            _, k, flow, piece = key
            src = store.at[slot_k[k], piece]
            dst = store.at[CROSS + (2 if flow == 0 else 0) * 4 + k, piece]
            there = at_x(step_of[flow])
        elif kind == "xf":
            _, k, flow = key
            src = store.at[CROSS + (2 if flow == 0 else 0) * 4 + k, flow]
            dst = store.at[CROSS + 1 * 4 + k, flow]
            there = at_x(step_of[flow])
        elif kind == "y":
            _, h, flow, piece = key
            half = (near, far)[h]
            src = half.at[0, piece]
            dst = half.at[(3 if flow == 0 else 1) * 2, piece]
            there = at_y(step_of[flow])
        elif kind == "yf":
            _, h, flow = key
            half = (near, far)[h]
            src = half.at[(3 if flow == 0 else 1) * 2, flow]
            dst = half.at[2 * 2, flow]
            there = at_y(step_of[flow])
        else:
            _, h, dy, piece = key
            half = (near, far)[h]
            src = half.at[dy * 2, piece]
            dst = half.at[dy * 2 + 1, piece]
            there = partner
        return pltpu.make_async_remote_copy(
            src_ref=src,
            dst_ref=dst,
            send_sem=send_sem.at[i],
            recv_sem=recv_sem.at[i],
            device_id=there,
            device_id_type=MESH,
        )

    def send(*key):
        copy = descriptor(key)
        copy.start()
        started.append(copy)

    def got(*key):
        descriptor(key).wait_recv()

    def send_unit(kind, at):
        for i in (0, 1):
            send(kind, at, 0, i)
            send(kind, at, 1, 1 - i)

    def chunk(n, half, unit, there):
        rows_ref = (near, far)[half]
        side = zh if half == 0 else 1 - zh

        def one(i, carry):
            place = ((y + i // 2) % 4) * 2 + (core + i % 2) % 2
            upper = side * 8 + place
            at = there * GRID + upper
            p = pick[at]
            dims = (((1,), (1,)), ((), ()))
            both = lax.dot_general(
                rows_ref[i, 0, p],
                store[unit, 1].reshape(UNIT, DEPTH),
                dims,
                preferred_element_type=jnp.float32,
            ) + lax.dot_general(
                rows_ref[i, 1, p],
                store[unit, 0].reshape(UNIT, DEPTH),
                dims,
                preferred_element_type=jnp.float32,
            )
            second = jnp.broadcast_to(side_of[at], (BLOCK, BLOCK)) > 0.5
            kept = jnp.where(second, both[:, BLOCK:], both[:, :BLOCK])
            below = gaps[pick[CELLS + at]] + gcol[pick[2 * CELLS + at]]
            stage[n, place] = (kept / below).astype(jnp.bfloat16)
            return carry

        lax.fori_loop(0, 8, one, 0)
        pltpu.make_async_copy(stage.at[n], dense.at[pl.ds(there * GRID + side * 8, 8)], out_sem.at[n]).start()
        outs.append((n, there, side))

    outs = []
    count = iter(range(32))

    def compute(half, k, dx):
        unit = slot_k[k] if dx == 0 else CROSS + (dx - 1) * 4 + k
        chunk(next(count), half, unit, line_k[k] * 4 + (x + dx) % 4)

    def half_ready(h):
        for dy in range(4):
            for piece in (0, 1):
                got("c", h, dy, piece)

    for i in (0, 1):
        send("z", 0, 1, i)
        send("z", 1, 1, 1 - i)
        send("x", 0, 0, i)
        send("x", 0, 1, 1 - i)
        send("y", 0, 0, i)
        send("y", 0, 1, 1 - i)
    send("c", 0, 0, 0)
    send("c", 0, 0, 1)
    for u in range(32):
        gaps[u] = jnp.broadcast_to(grow[:, u : u + 1], (BLOCK, BLOCK))
    stage[32] = jnp.zeros((8, BLOCK, BLOCK), jnp.bfloat16)
    zero = pltpu.make_async_copy(stage.at[32], dense.at[pl.ds(CELLS, 8)], local_sem.at[4])
    zero.start()
    for flow in (0, 1):
        got("z", flow, 1, flow)
        send("z", flow, 2, flow)
        got("x", 0, flow, flow)
        send("xf", 0, flow)
        got("y", 0, flow, flow)
        send("yf", 0, flow)
    for flow in (0, 1):
        got("z", flow, 1, 1 - flow)
        send("z", flow, 2, 1 - flow)
    send_unit("x", 1)
    for flow in (0, 1):
        got("y", 0, flow, 1 - flow)
    for dy in (1, 3):
        send("c", 0, dy, 0)
        send("c", 0, dy, 1)
    for flow in (0, 1):
        got("z", flow, 2, flow)
        send("z", flow, 3, flow)
    for flow in (0, 1):
        got("yf", 0, flow)
        send("c", 0, 2, flow)
    half_ready(0)
    compute(0, 0, 0)
    for flow in (0, 1):
        got("z", flow, 2, 1 - flow)
        send("z", flow, 3, 1 - flow)
    send_unit("x", 2)
    for flow in (0, 1):
        got("x", 1, flow, flow)
        send("xf", 1, flow)
    for flow in (0, 1):
        got("x", 0, flow, 1 - flow)
    compute(0, 0, 1)
    compute(0, 0, 3)
    for flow in (0, 1):
        got("z", flow, 3, flow)
        send("z", flow, 4, flow)
    for flow in (0, 1):
        got("xf", 0, flow)
    compute(0, 0, 2)
    compute(0, 1, 0)
    for flow in (0, 1):
        got("z", flow, 3, 1 - flow)
    send_unit("x", 3)
    for flow in (0, 1):
        got("x", 1, flow, 1 - flow)
    compute(0, 1, 1)
    compute(0, 1, 3)
    for flow in (0, 1):
        got("z", flow, 4, flow)
    send_unit("y", 1)
    send("c", 1, 0, 0)
    send("c", 1, 0, 1)
    for flow in (0, 1):
        got("x", 2, flow, flow)
        send("xf", 2, flow)
    for flow in (0, 1):
        got("xf", 1, flow)
    compute(0, 1, 2)
    compute(0, 2, 0)
    for flow in (0, 1):
        got("y", 1, flow, flow)
        send("yf", 1, flow)
    for flow in (0, 1):
        got("x", 2, flow, 1 - flow)
    compute(0, 2, 1)
    compute(0, 2, 3)
    for flow in (0, 1):
        got("y", 1, flow, 1 - flow)
    for dy in (1, 3):
        send("c", 1, dy, 0)
        send("c", 1, dy, 1)
    for flow in (0, 1):
        got("xf", 2, flow)
    compute(0, 2, 2)
    compute(0, 3, 0)
    for flow in (0, 1):
        got("x", 3, flow, flow)
        send("xf", 3, flow)
    for flow in (0, 1):
        got("yf", 1, flow)
        send("c", 1, 2, flow)
    half_ready(1)
    for k in range(4):
        compute(1, k, 0)
    for k in range(3):
        for dx in (1, 3, 2):
            compute(1, k, dx)
    for flow in (0, 1):
        got("x", 3, flow, 1 - flow)
    for dx in (1, 3):
        compute(0, 3, dx)
        compute(1, 3, dx)
    for flow in (0, 1):
        got("xf", 3, flow)
    compute(0, 3, 2)
    compute(1, 3, 2)

    for copy in started:
        copy.wait_send()
    zero.wait()
    for n, there, side in outs:
        pltpu.make_async_copy(stage.at[n], dense.at[pl.ds(there * GRID + side * 8, 8)], out_sem.at[n]).wait()


def products(pick, amplitudes, integrals, side_of, grow, gcol):
    anywhere = pl.BlockSpec(memory_space=pl.ANY)
    vmem = pl.BlockSpec(memory_space=pltpu.VMEM)
    pairs = len(KEYS)
    return pl.pallas_call(
        exchange,
        out_shape=jax.ShapeDtypeStruct((CELLS + 8, BLOCK, BLOCK), jnp.bfloat16),
        in_specs=[pl.BlockSpec(memory_space=pltpu.SMEM), anywhere, anywhere, vmem, vmem, vmem],
        out_specs=anywhere,
        scratch_shapes=[
            pltpu.VMEM((UNITS, 2, 2, BLOCK, DEPTH), jnp.bfloat16),
            pltpu.VMEM((8, 2, 2, BLOCK, DEPTH), jnp.bfloat16),
            pltpu.VMEM((8, 2, 2, BLOCK, DEPTH), jnp.bfloat16),
            pltpu.VMEM((32, BLOCK, BLOCK), jnp.float32),
            pltpu.VMEM((33, 8, BLOCK, BLOCK), jnp.bfloat16),
            pltpu.SemaphoreType.DMA((5,)),
            pltpu.SemaphoreType.DMA((pairs,)),
            pltpu.SemaphoreType.DMA((pairs,)),
            pltpu.SemaphoreType.DMA((32,)),
        ],
        compiler_params=pltpu.CompilerParams(
            collective_id=0, has_side_effects=True, vmem_limit_bytes=60 * 1024 * 1024
        ),
        name="exchange",
    )(pick, amplitudes, integrals, side_of, grow, gcol)


def ordered(places, dense, out, held, in_sem, out_sem):
    group = 16
    groups = TILES // group

    def read(g, j):
        return pltpu.make_async_copy(dense.at[places[g * group + j]], held.at[g * group + j], in_sem.at[g * group + j])

    def write(g):
        rows = pl.ds(g * group, group)
        return pltpu.make_async_copy(held.at[rows], out.at[0, 0, rows], out_sem.at[g])

    for g in range(groups):
        for j in range(group):
            read(g, j).start()
    for g in range(groups):
        for j in range(group):
            read(g, j).wait()
        write(g).start()
    for g in range(groups):
        write(g).wait()


def in_order(places, dense):
    anywhere = pl.BlockSpec(memory_space=pl.ANY)
    return pl.pallas_call(
        ordered,
        out_shape=jax.ShapeDtypeStruct((1, 1, TILES, BLOCK, BLOCK), jnp.bfloat16),
        in_specs=[pl.BlockSpec(memory_space=pltpu.SMEM), anywhere],
        out_specs=anywhere,
        scratch_shapes=[
            pltpu.VMEM((TILES, BLOCK, BLOCK), jnp.bfloat16),
            pltpu.SemaphoreType.DMA((TILES,)),
            pltpu.SemaphoreType.DMA((12,)),
        ],
        name="ordered",
    )(places, dense)


def shards(amplitudes, integrals, block_mask, occ_energy, vir_energy):
    row, col = lax.axis_index("row"), lax.axis_index("col")
    cell = lax.dynamic_index_in_dim(block_mask.reshape(32, GRID, GRID, 2), col, 2, keepdims=False)
    four = cell.reshape(GRID, 2, GRID, 2)
    low = jnp.max(four[:, 1], axis=2).T
    right = jnp.max(four[..., 1], axis=1).T
    line = jnp.arange(GRID, dtype=jnp.int32)
    pick = jnp.stack([low, line[None, :] * 2 + low, line[:, None] * 2 + right]).reshape(3 * CELLS)
    side_of = jnp.broadcast_to(right.astype(jnp.float32).reshape(CELLS, 1, 1), (CELLS, 1, BLOCK))

    flat = cell.reshape(32, 32).astype(jnp.float32)
    at = jnp.arange(32)
    inside = flat @ (at[:, None] <= at[None, :]).astype(jnp.float32)
    ahead = (at[None, :] < at[:, None]).astype(jnp.float32) @ inside[:, 31:]
    ranks = (inside + ahead).astype(jnp.int32).reshape(1024)
    slot = jnp.arange(TILES, dtype=jnp.int32)
    where = jnp.sum((ranks[None, :] <= slot[:, None]).astype(jnp.int32), axis=1)
    dense_at = (where % 32) // 2 * GRID + where // 64
    places = jnp.where(slot < ranks[1023], dense_at, CELLS)

    blocks = row * 32 + jnp.arange(32, dtype=jnp.int32)
    levels = vir_energy.reshape(8, BLOCK)
    grow = (levels[blocks % 8] - occ_energy[blocks // 8][:, None]).T
    blocks = (jnp.arange(32, dtype=jnp.int32) // 2 * GRID + col) * 2 + jnp.arange(32, dtype=jnp.int32) % 2
    gcol = (levels[blocks % 8] - occ_energy[blocks // 8][:, None]).reshape(32, 1, BLOCK)

    dense = products(
        pick, amplitudes.reshape(2, BLOCK, DEPTH), integrals.reshape(2, BLOCK, DEPTH), side_of, grow, gcol
    )
    return in_order(places, dense)


def solution(mesh):
    in_specs = (P(("row", "col"), None), P(("row", "col"), None), P("row", None), P(), P())
    out_specs = P("row", "col", None, None, None)
    return jax.shard_map(shards, mesh=mesh, in_specs=in_specs, out_specs=out_specs, check_vma=False)
```

time: 927 us -> 203 us (0.22)
  the two profiles are of different devices: /device:TPU:89 before, /device:TPU:27 now
where the time goes in v1:
time: 203 us; the launch traced here: 201 us
  Pallas kernels  189 us (93%)
  local copies, waits for them, and re-layouts  8.33 us (4%)
  other arithmetic  2.99 us (1%)
    pallas_call x1, Pallas kernels, products(): pl.pallas_call(exchange, out_shape=jax.ShapeDtypeStruct((CELLS + 8, BLOCK...  173 us
    pallas_call x1, Pallas kernels, in_order(): pl.pallas_call(ordered, out_shape=jax.ShapeDtypeStruct((1, 1, TILES, BLOC...  16.9 us

profile of v1, /device:TPU:27, one launch (start us, length us, event | category | flops | bytes accessed | tf_op | source)
XLA Modules:
  0.0 201.2 jit_solution(9288588896098092336)
XLA Ops:
  0.0 0.0 copy-start
  0.0 0.7 copy-done
  0.8 1.4 gather_fusion.1
  2.1 1.4 gather_fusion.3
  3.5 0.6 gather_fusion.2
  4.1 0.7 broadcast_subtract_fusion.gcol
  4.8 0.6 gather_fusion
  5.3 0.1 copy.37
  5.4 0.6 subtract_bitcast_fusion.grow
  6.1 1.0 copy.31
  7.1 0.2 fusion
  7.3 0.1 convolution_bitcast_fusion
  7.4 0.1 copy.32
  7.5 0.1 reshape.310
  7.5 0.6 slice.13
  8.1 0.2 convert_reduce_fusion
  8.3 1.3 compare_select_fusion.4.places
  9.6 0.1 copy.33
  9.7 0.1 fusion.1
  9.8 0.1 copy.36
  9.9 0.1 broadcast_in_dim.8
  10.0 0.1 copy.35
  10.0 0.7 reshape.312.pick
  10.7 1.0 broadcast_in_dim.9.side_of
  11.7 172.5 %exchange.1.dense = bf16[264,128,128]{2,1,0:T(8,128)(2,1)} custom-call(s32[768]{0:T(1024)} %reshape.312.pick, bf16[2,128,768]{2,1,0:T(8,128)(2,1)} %bitcast.38, bf16[2,128,768]{2,1,0:T(8,128)(2,1)} %bitcast.39, f32[256,1,128]{2,1,0:T(1,128)} %broadcast_in_dim.9.side_of, f32[128,32]{1,0:T(8,128)} %subtract_bitcast_fusion.grow, ...), custom_call_target="tpu_custom_call" | custom-call | tf_op jit(solution)/shard_map/exchange/pallas_call | solution.py:320
  184.3 16.9 %ordered.1 = bf16[1,1,192,128,128]{4,3,2,1,0:T(8,128)(2,1)} custom-call(s32[192]{0:T(256)} %compare_select_fusion.4.places, bf16[264,128,128]{2,1,0:T(8,128)(2,1)} %exchange.1.dense), custom_call_target="tpu_custom_call" | custom-call | tf_op jit(solution)/shard_map/ordered/pallas_call | solution.py:367
  (13 shorter events, 0.2 us)
Async XLA Ops:
  0.0 0.7 copy-start

commit v2 on v1

v2 whole, which is shorter than its diff:
```python
import functools

import jax
import jax.numpy as jnp
from jax import lax
from jax.experimental import pallas as pl
from jax.experimental.pallas import tpu as pltpu
from jax.sharding import PartitionSpec as P

BLOCK = 128
UNIT = 256
DEPTH = 768
TILES = 192
GRID = 16
CELLS = GRID * GRID
MESH = pl.DeviceIdType.MESH

OWN = 6
CROSS = 7
UNITS = 19
LIMIT = 46 * 1024 * 1024


def table(at, values):
    out = jnp.int32(values[0])
    for i in range(1, len(values)):
        out = jnp.where(at == i, jnp.int32(values[i]), out)
    return out


def names():
    keys = []
    for flow in (0, 1):
        for dist in (1, 2, 3):
            for piece in (0, 1):
                keys.append(("z", flow, dist, piece))
        keys.append(("z", flow, 4, flow))
    for k in range(4):
        for flow in (0, 1):
            for piece in (0, 1):
                keys.append(("x", k, flow, piece))
            keys.append(("xf", k, flow))
    for h in (0, 1):
        for flow in (0, 1):
            for piece in (0, 1):
                keys.append(("y", h, flow, piece))
            keys.append(("yf", h, flow))
        for dy in range(4):
            for piece in (0, 1):
                keys.append(("c", h, dy, piece))
    return {key: i for i, key in enumerate(keys)}


KEYS = names()


def exchange(
    low_s, amp, ints, side_of, occ, vir_all, dense,
    store, near, far, last, gaps, vir, occ_s,
    local_sem, send_sem, recv_sem,
):
    row, col = lax.axis_index("row"), lax.axis_index("col")
    zl, x = row // 4, row % 4
    zh, y, core = col // 8, (col // 2) % 4, col % 2
    z = zh * 4 + zl

    def at_x(step):
        return (zl * 4 + (x + step) % 4, col)

    def at_y(step):
        return (row, zh * 8 + ((y + step) % 4) * 2 + core)

    def at_z(step):
        there = (z + step) % 8
        return ((there % 4) * 4 + x, (there // 4) * 8 + y * 2 + core)

    partner = (row, zh * 8 + y * 2 + (1 - core))
    step_of = (1, 3)
    ring_of = (1, 7)

    own_copies = []
    for piece, src in enumerate((amp, ints)):
        own_copies.append(pltpu.make_async_copy(src, near.at[0, piece], local_sem.at[piece]))
        own_copies.append(pltpu.make_async_copy(src, store.at[OWN, piece], local_sem.at[2 + piece]))
    for copy in own_copies:
        copy.start()
    occ_copy = pltpu.make_async_copy(occ, occ_s, local_sem.at[5])
    occ_copy.start()
    vir_copy = pltpu.make_async_copy(vir_all, vir, local_sem.at[7])
    vir_copy.start()

    barrier = pltpu.get_barrier_semaphore()
    for there in (at_x(1), at_x(3), at_y(1), at_y(3), at_z(1), at_z(7), partner):
        pl.semaphore_signal(barrier, inc=1, device_id=there, device_id_type=MESH)
    pl.semaphore_wait(barrier, 7)
    for copy in (*own_copies, vir_copy):
        copy.wait()

    slot_k = [OWN] + [table(zl, v) for v in ((3, 0, 3, 0), (4, 3, 0, 1), (5, 4, 1, 2))]
    line_k = [zl] + [table(zl, v) for v in ((1, 0, 3, 2), (2, 2, 1, 1), (3, 3, 0, 0))]

    def rows_at(h, dy, dc, piece):
        if h == 0:
            return near.at[dy * 2 + dc, piece]
        return last.at[dc, piece] if dy == 2 else far.at[(0, 1, 0, 2)[dy] * 2 + dc, piece]

    started = []

    def descriptor(key):
        i = KEYS[key]
        kind = key[0]
        if kind == "z":
            _, flow, dist, piece = key
            src = rows_at(0, 0, 0, piece) if dist == 1 else store.at[flow * 3 + dist - 2, piece]
            dst = rows_at(1, 0, 0, piece) if dist == 4 else store.at[flow * 3 + dist - 1, piece]
            there = at_z(ring_of[flow])
        elif kind == "x":
            _, k, flow, piece = key
            src = store.at[slot_k[k], piece]
            dst = store.at[CROSS + (2 if flow == 0 else 0) * 4 + k, piece]
            there = at_x(step_of[flow])
        elif kind == "xf":
            _, k, flow = key
            src = store.at[CROSS + (2 if flow == 0 else 0) * 4 + k, flow]
            dst = store.at[CROSS + 1 * 4 + k, flow]
            there = at_x(step_of[flow])
        elif kind == "y":
            _, h, flow, piece = key
            src = rows_at(h, 0, 0, piece)
            dst = rows_at(h, 3 if flow == 0 else 1, 0, piece)
            there = at_y(step_of[flow])
        elif kind == "yf":
            _, h, flow = key
            src = rows_at(h, 3 if flow == 0 else 1, 0, flow)
            dst = rows_at(h, 2, 0, flow)
            there = at_y(step_of[flow])
        else:
            _, h, dy, piece = key
            src = rows_at(h, dy, 0, piece)
            dst = rows_at(h, dy, 1, piece)
            there = partner
        return pltpu.make_async_remote_copy(
            src_ref=src,
            dst_ref=dst,
            send_sem=send_sem.at[i],
            recv_sem=recv_sem.at[i],
            device_id=there,
            device_id_type=MESH,
        )

    def send(*key):
        copy = descriptor(key)
        copy.start()
        started.append(copy)

    def got(*key):
        descriptor(key).wait_recv()

    def send_unit(kind, at):
        for i in (0, 1):
            send(kind, at, 0, i)
            send(kind, at, 1, 1 - i)

    groups = (
        (near, 0, [(dy, dc) for dy in range(4) for dc in (0, 1)]),
        (far, 1, [(dy, dc) for dy in (0, 1, 3) for dc in (0, 1)]),
        (last, 1, [(2, dc) for dc in (0, 1)]),
    )
    first_line = vir[pl.ds((2 * col) % 8, 1), :]
    second_line = vir[pl.ds((2 * col + 1) % 8, 1), :]

    def chunk(group, k, dx):
        rows_ref, half, members = groups[group]
        unit = slot_k[k] if dx == 0 else CROSS + (dx - 1) * 4 + k
        there = line_k[k] * 4 + (x + dx) % 4
        side = zh if half == 0 else 1 - zh
        places = [((y + dy) % 4) * 2 + (core + dc) % 2 for dy, dc in members]
        ats = [there * GRID + side * 8 + p for p in places]
        lows = [low_s[at] for at in ats]
        dims = (((1,), (1,)), ((), ()))
        both = [
            lax.dot_general(
                jnp.concatenate([rows_ref[i, piece, low] for i, low in enumerate(lows)], axis=0),
                store[unit, 1 - piece].reshape(UNIT, DEPTH),
                dims,
                preferred_element_type=jnp.float32,
            )
            for piece in (0, 1)
        ]
        both = both[0] + both[1]
        level = occ_s[there * 4 + col // 4]
        for i, (place, at) in enumerate(zip(places, ats)):
            mine = both[i * BLOCK : (i + 1) * BLOCK]
            right = side_of[at]
            across = jnp.where(right > 0.5, second_line, first_line) - level
            kept = jnp.where(jnp.broadcast_to(right, (BLOCK, BLOCK)) > 0.5, mine[:, BLOCK:], mine[:, :BLOCK])
            below = gaps[(side * 8 + place) * 2 + lows[i]] + across
            dense[at] = (kept / below).astype(jnp.bfloat16)

    def compute(group, *todo):
        for first, step, count in todo:
            for at in range(first, first + step * count, step):
                chunk(group, at // 4, at % 4)

    def half_ready(h, dys):
        for dy in dys:
            for piece in (0, 1):
                got("c", h, dy, piece)

    for i in (0, 1):
        send("z", 0, 1, i)
        send("z", 1, 1, 1 - i)
        send("x", 0, 0, i)
        send("x", 0, 1, 1 - i)
        send("y", 0, 0, i)
        send("y", 0, 1, 1 - i)
    send("c", 0, 0, 0)
    send("c", 0, 0, 1)
    occ_copy.wait()
    for j in range(8):
        turned = jnp.broadcast_to(vir[j : j + 1, :], (BLOCK, BLOCK)).T
        for t in range(4):
            gaps[j + 8 * t] = turned - occ_s[row * 4 + t]
    dense[CELLS] = jnp.zeros((BLOCK, BLOCK), jnp.bfloat16)
    for flow in (0, 1):
        got("z", flow, 1, flow)
        send("z", flow, 2, flow)
        got("x", 0, flow, flow)
        send("xf", 0, flow)
        got("y", 0, flow, flow)
        send("yf", 0, flow)
    for flow in (0, 1):
        got("z", flow, 1, 1 - flow)
        send("z", flow, 2, 1 - flow)
    send_unit("x", 1)
    for flow in (0, 1):
        got("y", 0, flow, 1 - flow)
    for dy in (1, 3):
        send("c", 0, dy, 0)
        send("c", 0, dy, 1)
    for flow in (0, 1):
        got("z", flow, 2, flow)
        send("z", flow, 3, flow)
    for flow in (0, 1):
        got("yf", 0, flow)
        send("c", 0, 2, flow)
    half_ready(0, range(4))
    compute(0, (0, 1, 1))
    for flow in (0, 1):
        got("z", flow, 2, 1 - flow)
        send("z", flow, 3, 1 - flow)
    send_unit("x", 2)
    for flow in (0, 1):
        got("x", 1, flow, flow)
        send("xf", 1, flow)
    for flow in (0, 1):
        got("x", 0, flow, 1 - flow)
    compute(0, (1, 2, 2))
    for flow in (0, 1):
        got("z", flow, 3, flow)
        send("z", flow, 4, flow)
    for flow in (0, 1):
        got("xf", 0, flow)
    compute(0, (2, 2, 2))
    for flow in (0, 1):
        got("z", flow, 3, 1 - flow)
    send_unit("x", 3)
    for flow in (0, 1):
        got("x", 1, flow, 1 - flow)
    compute(0, (5, 2, 2))
    for flow in (0, 1):
        got("z", flow, 4, flow)
    send_unit("y", 1)
    send("c", 1, 0, 0)
    send("c", 1, 0, 1)
    for flow in (0, 1):
        got("x", 2, flow, flow)
        send("xf", 2, flow)
    for flow in (0, 1):
        got("xf", 1, flow)
    compute(0, (6, 2, 2))
    for flow in (0, 1):
        got("y", 1, flow, flow)
        send("yf", 1, flow)
    for flow in (0, 1):
        got("x", 2, flow, 1 - flow)
    compute(0, (9, 2, 2))
    for flow in (0, 1):
        got("y", 1, flow, 1 - flow)
    for dy in (1, 3):
        send("c", 1, dy, 0)
        send("c", 1, dy, 1)
    for flow in (0, 1):
        got("xf", 2, flow)
    compute(0, (10, 2, 2))
    half_ready(1, (0, 1, 3))
    compute(1, (0, 1, 6))
    for flow in (0, 1):
        got("x", 3, flow, flow)
        send("xf", 3, flow)
    for flow in (0, 1):
        got("yf", 1, flow)
        send("c", 1, 2, flow)
    compute(1, (6, 1, 7))
    half_ready(1, (2,))
    compute(2, (0, 1, 13))
    for flow in (0, 1):
        got("x", 3, flow, 1 - flow)
    for group in range(3):
        compute(group, (13, 2, 2))
    for flow in (0, 1):
        got("xf", 3, flow)
    for group in range(3):
        compute(group, (14, 2, 1))

    for copy in started:
        copy.wait_send()


def products(low, amplitudes, integrals, side_of, occ_energy, vir_energy):
    anywhere = pl.BlockSpec(memory_space=pl.ANY)
    vmem = pl.BlockSpec(memory_space=pltpu.VMEM)
    pairs = len(KEYS)
    return pl.pallas_call(
        exchange,
        out_shape=pltpu.VMEM((CELLS + 8, BLOCK, BLOCK), jnp.bfloat16),
        in_specs=[pl.BlockSpec(memory_space=pltpu.SMEM), anywhere, anywhere, vmem, anywhere, anywhere],
        out_specs=vmem,
        scratch_shapes=[
            pltpu.VMEM((UNITS, 2, 2, BLOCK, DEPTH), jnp.bfloat16),
            pltpu.VMEM((8, 2, 2, BLOCK, DEPTH), jnp.bfloat16),
            pltpu.VMEM((6, 2, 2, BLOCK, DEPTH), jnp.bfloat16),
            pltpu.VMEM((2, 2, 2, BLOCK, DEPTH), jnp.bfloat16),
            pltpu.VMEM((32, BLOCK, BLOCK), jnp.float32),
            pltpu.VMEM(vir_energy.shape, jnp.float32),
            pltpu.SMEM(occ_energy.shape, jnp.float32),
            pltpu.SemaphoreType.DMA((8,)),
            pltpu.SemaphoreType.DMA((pairs,)),
            pltpu.SemaphoreType.DMA((pairs,)),
        ],
        compiler_params=pltpu.CompilerParams(
            collective_id=0, has_side_effects=True, vmem_limit_bytes=LIMIT
        ),
        name="exchange",
    )(low, amplitudes, integrals, side_of, occ_energy, vir_energy)


def ordered(ranks, dense, out, sem):
    def put(src, slot):
        pltpu.make_async_copy(dense.at[src], out.at[0, 0, slot], sem.at[0]).start()

    def some(t, carry):
        for i in range(8):
            at = t * 8 + i
            rank = ranks[at]

            @pl.when(rank > 0)
            def _():
                put(at, rank - 1)

        return carry

    lax.fori_loop(0, CELLS // 8, some, 0)

    def rest(slot, carry):
        put(CELLS, slot)
        return carry

    lax.fori_loop(ranks[CELLS], TILES, rest, 0)
    whole = dense.at[pl.ds(0, TILES)]
    pltpu.make_async_copy(whole, out.at[0, 0], sem.at[0]).wait()


def in_order(ranks, dense):
    anywhere = pl.BlockSpec(memory_space=pl.ANY)
    return pl.pallas_call(
        ordered,
        out_shape=jax.ShapeDtypeStruct((1, 1, TILES, BLOCK, BLOCK), jnp.bfloat16),
        in_specs=[pl.BlockSpec(memory_space=pltpu.SMEM), anywhere],
        out_specs=anywhere,
        scratch_shapes=[pltpu.SemaphoreType.DMA((1,))],
        compiler_params=pltpu.CompilerParams(vmem_limit_bytes=1024 * 1024),
        name="ordered",
    )(ranks, dense)


def shards(amplitudes, integrals, block_mask, occ_energy, vir_energy):
    col = lax.axis_index("col")
    cell = lax.dynamic_index_in_dim(block_mask.reshape(32, GRID, GRID, 2), col, 2, keepdims=False)
    four = cell.reshape(GRID, 2, GRID, 2)
    low = jnp.sum(four[:, 1], axis=2).T.reshape(CELLS)
    right = jnp.sum(four[..., 1], axis=1).T
    side_of = jnp.broadcast_to(right.astype(jnp.float32).reshape(CELLS, 1, 1), (CELLS, 1, BLOCK))
    flat = cell.reshape(32, 32).astype(jnp.float32)
    at = jnp.arange(32)
    inside = flat @ (at[:, None] <= at[None, :]).astype(jnp.float32)
    ahead = (at[None, :] < at[:, None]).astype(jnp.float32) @ inside[:, 31:]
    upto = inside + ahead
    ranks = jnp.sum((flat * upto).reshape(GRID, 2, GRID, 2), axis=(1, 3)).T.reshape(CELLS)
    ranks = jnp.concatenate([ranks, jnp.broadcast_to(upto[31, 31:], (CELLS,))]).astype(jnp.int32)
    dense = products(
        low,
        amplitudes.reshape(2, BLOCK, DEPTH),
        integrals.reshape(2, BLOCK, DEPTH),
        side_of,
        occ_energy,
        vir_energy.reshape(8, BLOCK),
    )
    return in_order(ranks, dense)


def solution(mesh):
    in_specs = (P(("row", "col"), None), P(("row", "col"), None), P("row", None), P(), P())
    out_specs = P("row", "col", None, None, None)
    return jax.shard_map(shards, mesh=mesh, in_specs=in_specs, out_specs=out_specs, check_vma=False)
```

time: 203 us -> 133 us (0.66)
  the two profiles are of different devices: /device:TPU:27 before, /device:TPU:1 now
where the time goes in v2:
time: 133 us
  Pallas kernels  128 us (96%)
  local copies, waits for them, and re-layouts  3.9 us (3%)
    pallas_call x1, Pallas kernels, products(): pl.pallas_call(exchange, out_shape=pltpu.VMEM((CELLS + 8, BLOCK, BLOCK),...  125 us
    pallas_call x1, Pallas kernels, in_order(): pl.pallas_call(ordered, out_shape=jax.ShapeDtypeStruct((1, 1, TILES, BLOC...  3.14 us

profile of v2, /device:TPU:1, one launch (start us, length us, event | category | flops | bytes accessed | tf_op | source)
XLA Modules:
  0.0 133.1 jit_solution(16427480814164109238)
XLA Ops:
  0.0 1.0 copy.10
  1.0 0.2 fusion
  1.2 0.1 convolution_bitcast_fusion
  1.3 0.6 slice.17
  1.9 0.1 copy.11
  2.0 0.1 copy.13
  2.1 0.1 copy.14
  2.2 0.7 reshape.43.low_s
  2.9 0.1 copy.15
  3.0 0.1 broadcast_in_dim.7
  3.0 1.0 broadcast_in_dim.8.side_of
  4.0 0.2 reshape.40
  4.2 0.1 reduce_sum.27
  4.3 0.1 copy.12
  4.4 0.1 reshape.41
  4.5 0.6 pad_convert_fusion.ranks
  5.1 124.7 %exchange.1.dense = bf16[264,128,128]{2,1,0:T(8,128)(2,1)S(1)} custom-call(s32[256]{0:T(256)} %reshape.43.low_s, bf16[2,128,768]{2,1,0:T(8,128)(2,1)} %bitcast.15, bf16[2,128,768]{2,1,0:T(8,128)(2,1)} %bitcast.16, f32[256,1,128]{2,1,0:T(1,128)} %broadcast_in_dim.8.side_of, f32[64]{0:T(128)} %occ.1, f32[8,128]{1,0:T(8,128)} %bitcast.24), custom_call_target="tpu_custom_call" | custom-call | tf_op jit(solution)/shard_map/exchange/pallas_call | solution.py:324
  129.8 3.1 %ordered.1 = bf16[1,1,192,128,128]{4,3,2,1,0:T(8,128)(2,1)} custom-call(s32[512]{0:T(512)S(1)} %pad_convert_fusion.ranks, bf16[264,128,128]{2,1,0:T(8,128)(2,1)S(1)} %exchange.1.dense), custom_call_target="tpu_custom_call" | custom-call | tf_op jit(solution)/shard_map/ordered/pallas_call | solution.py:376
  (5 shorter events, 0.1 us)

commit v3 on v2

--- a/solution.py
+++ b/solution.py
@@ -48,10 +48,15 @@
         for dy in range(4):
             for piece in (0, 1):
                 keys.append(("c", h, dy, piece))
+    for flow in (0, 1):
+        for dist in (1, 2, 3):
+            for piece in (0, 1):
+                keys.append(("w", flow, dist, piece))
     return {key: i for i, key in enumerate(keys)}
 
 
 KEYS = names()
+LINES = ((0, 1, 2, 3), (1, 0, 2, 3), (2, 3, 1, 0), (3, 2, 1, 0))
 
 
 def exchange(
@@ -97,14 +102,30 @@
         copy.wait()
 
     slot_k = [OWN] + [table(zl, v) for v in ((3, 0, 3, 0), (4, 3, 0, 1), (5, 4, 1, 2))]
-    line_k = [zl] + [table(zl, v) for v in ((1, 0, 3, 2), (2, 2, 1, 1), (3, 3, 0, 0))]
+    line_k = [zl] + [table(zl, [lines[k] for lines in LINES]) for k in (1, 2, 3)]
 
     def rows_at(h, dy, dc, piece):
         if h == 0:
             return near.at[dy * 2 + dc, piece]
         return last.at[dc, piece] if dy == 2 else far.at[(0, 1, 0, 2)[dy] * 2 + dc, piece]
 
+    def line_slot(flow, dist, ahead):
+        step = -1 if flow else 1
+        slots = []
+        for at in range(4):
+            there = at + step * ahead
+            line = there - step * dist
+            slots.append(LINES[there].index(line) if 0 <= there < 4 and 0 <= line < 4 else 0)
+        return table(zl, slots)
+
+    def passes_on(flow, dist):
+        return (zl >= dist - 1) & (zl <= 2) if flow == 0 else (zl <= 4 - dist) & (zl >= 1)
+
+    def takes(flow, dist):
+        return zl >= dist if flow == 0 else zl <= 3 - dist
+
     started = []
+    on_line = []
 
     def descriptor(key):
         i = KEYS[key]
@@ -123,7 +144,14 @@
             _, k, flow = key
             src = store.at[CROSS + (2 if flow == 0 else 0) * 4 + k, flow]
             dst = store.at[CROSS + 1 * 4 + k, flow]
+            if k > 0:
+                src, dst = src.at[0], dst.at[0]
             there = at_x(step_of[flow])
+        elif kind == "w":
+            _, flow, dist, piece = key
+            src = store.at[CROSS + 4 + line_slot(flow, dist - 1, 0), piece, 1]
+            dst = store.at[CROSS + 4 + line_slot(flow, dist, 1), piece, 1]
+            there = at_z(ring_of[flow])
         elif kind == "y":
             _, h, flow, piece = key
             src = rows_at(h, 0, 0, piece)
@@ -155,6 +183,24 @@
 
     def got(*key):
         descriptor(key).wait_recv()
+
+    def send_line(dist):
+        for flow in (0, 1):
+
+            @pl.when(passes_on(flow, dist))
+            def _(flow=flow):
+                for piece in (0, 1):
+                    descriptor(("w", flow, dist, piece)).start()
+
+            on_line.append((flow, dist))
+
+    def got_line(dist):
+        for flow in (0, 1):
+
+            @pl.when(takes(flow, dist))
+            def _(flow=flow):
+                for piece in (0, 1):
+                    descriptor(("w", flow, dist, piece)).wait_recv()
 
     def send_unit(kind, at):
         for i in (0, 1):
@@ -231,7 +277,6 @@
         send("yf", 0, flow)
     for flow in (0, 1):
         got("z", flow, 1, 1 - flow)
-        send("z", flow, 2, 1 - flow)
     send_unit("x", 1)
     for flow in (0, 1):
         got("y", 0, flow, 1 - flow)
@@ -241,30 +286,28 @@
     for flow in (0, 1):
         got("z", flow, 2, flow)
         send("z", flow, 3, flow)
+        send("z", flow, 2, 1 - flow)
     for flow in (0, 1):
         got("yf", 0, flow)
         send("c", 0, 2, flow)
     half_ready(0, range(4))
     compute(0, (0, 1, 1))
     for flow in (0, 1):
+        got("z", flow, 3, flow)
+        send("z", flow, 4, flow)
+    for flow in (0, 1):
+        got("x", 0, flow, 1 - flow)
+        got("x", 1, flow, flow)
+        send("xf", 1, flow)
+    compute(0, (1, 2, 2))
+    for flow in (0, 1):
         got("z", flow, 2, 1 - flow)
         send("z", flow, 3, 1 - flow)
     send_unit("x", 2)
     for flow in (0, 1):
-        got("x", 1, flow, flow)
-        send("xf", 1, flow)
-    for flow in (0, 1):
-        got("x", 0, flow, 1 - flow)
-    compute(0, (1, 2, 2))
-    for flow in (0, 1):
-        got("z", flow, 3, flow)
-        send("z", flow, 4, flow)
-    for flow in (0, 1):
         got("xf", 0, flow)
+    send_line(1)
     compute(0, (2, 2, 2))
-    for flow in (0, 1):
-        got("z", flow, 3, 1 - flow)
-    send_unit("x", 3)
     for flow in (0, 1):
         got("x", 1, flow, 1 - flow)
     compute(0, (5, 2, 2))
@@ -276,9 +319,10 @@
     for flow in (0, 1):
         got("x", 2, flow, flow)
         send("xf", 2, flow)
-    for flow in (0, 1):
-        got("xf", 1, flow)
-    compute(0, (6, 2, 2))
+    compute(0, (8, 1, 1))
+    for flow in (0, 1):
+        got("z", flow, 3, 1 - flow)
+    send_unit("x", 3)
     for flow in (0, 1):
         got("y", 1, flow, flow)
         send("yf", 1, flow)
@@ -290,9 +334,11 @@
     for dy in (1, 3):
         send("c", 1, dy, 0)
         send("c", 1, dy, 1)
-    for flow in (0, 1):
-        got("xf", 2, flow)
-    compute(0, (10, 2, 2))
+    got_line(1)
+    send_line(2)
+    for flow in (0, 1):
+        got("xf", 1, flow)
+    compute(0, (6, 6, 2))
     half_ready(1, (0, 1, 3))
     compute(1, (0, 1, 6))
     for flow in (0, 1):
@@ -301,6 +347,11 @@
     for flow in (0, 1):
         got("yf", 1, flow)
         send("c", 1, 2, flow)
+    got_line(2)
+    send_line(3)
+    for flow in (0, 1):
+        got("xf", 2, flow)
+    compute(0, (10, 1, 1))
     compute(1, (6, 1, 7))
     half_ready(1, (2,))
     compute(2, (0, 1, 13))
@@ -310,11 +361,18 @@
         compute(group, (13, 2, 2))
     for flow in (0, 1):
         got("xf", 3, flow)
+    got_line(3)
     for group in range(3):
         compute(group, (14, 2, 1))
 
     for copy in started:
         copy.wait_send()
+    for flow, dist in on_line:
+
+        @pl.when(passes_on(flow, dist))
+        def _(flow=flow, dist=dist):
+            for piece in (0, 1):
+                descriptor(("w", flow, dist, piece)).wait_send()
 
 
 def products(low, amplitudes, integrals, side_of, occ_energy, vir_energy):

time: 133 us -> 117 us (0.88)
  Pallas kernels: 128 us -> 112 us
    pallas_call x1, Pallas kernels: 125 us -> 109 us  [products(): pl.pallas_call(exchange, out_shape=pltpu.VMEM((CELLS + 8, BLOCK, BLOCK),...]
where the time goes in v3:
time: 117 us
  Pallas kernels  112 us (96%)
  local copies, waits for them, and re-layouts  3.9 us (3%)
    pallas_call x1, Pallas kernels, products(): pl.pallas_call(exchange, out_shape=pltpu.VMEM((CELLS + 8, BLOCK, BLOCK),...  109 us
    pallas_call x1, Pallas kernels, in_order(): pl.pallas_call(ordered, out_shape=jax.ShapeDtypeStruct((1, 1, TILES, BLOC...  3.14 us

profile of v3, /device:TPU:1, one launch (start us, length us, event | category | flops | bytes accessed | tf_op | source)
XLA Modules:
  0.0 117.0 jit_solution(8743605551085024123)
XLA Ops:
  0.0 1.0 copy.10
  1.0 0.2 fusion
  1.2 0.1 convolution_bitcast_fusion
  1.3 0.6 slice.17
  1.9 0.1 copy.11
  2.0 0.1 copy.13
  2.1 0.1 copy.14
  2.2 0.7 reshape.43.low_s
  2.9 0.1 copy.15
  3.0 0.1 broadcast_in_dim.7
  3.0 1.0 broadcast_in_dim.8.side_of
  4.0 0.2 reshape.40
  4.2 0.1 reduce_sum.27
  4.3 0.1 copy.12
  4.4 0.1 reshape.41
  4.5 0.6 pad_convert_fusion.ranks
  5.1 108.6 %exchange.1.dense = bf16[264,128,128]{2,1,0:T(8,128)(2,1)S(1)} custom-call(s32[256]{0:T(256)} %reshape.43.low_s, bf16[2,128,768]{2,1,0:T(8,128)(2,1)} %bitcast.15, bf16[2,128,768]{2,1,0:T(8,128)(2,1)} %bitcast.16, f32[256,1,128]{2,1,0:T(1,128)} %broadcast_in_dim.8.side_of, f32[64]{0:T(128)} %occ.1, f32[8,128]{1,0:T(8,128)} %bitcast.24), custom_call_target="tpu_custom_call" | custom-call | tf_op jit(solution)/shard_map/exchange/pallas_call | solution.py:382
  113.7 3.1 %ordered.1 = bf16[1,1,192,128,128]{4,3,2,1,0:T(8,128)(2,1)} custom-call(s32[512]{0:T(512)S(1)} %pad_convert_fusion.ranks, bf16[264,128,128]{2,1,0:T(8,128)(2,1)S(1)} %exchange.1.dense), custom_call_target="tpu_custom_call" | custom-call | tf_op jit(solution)/shard_map/ordered/pallas_call | solution.py:434
  (5 shorter events, 0.1 us)

commit v4 on v3

--- a/solution.py
+++ b/solution.py
@@ -60,7 +60,7 @@
 
 
 def exchange(
-    low_s, amp, ints, side_of, occ, vir_all, dense,
+    sides, amp, ints, occ, vir_all, dense,
     store, near, far, last, gaps, vir, occ_s,
     local_sem, send_sem, recv_sem,
 ):
@@ -220,9 +220,8 @@
         unit = slot_k[k] if dx == 0 else CROSS + (dx - 1) * 4 + k
         there = line_k[k] * 4 + (x + dx) % 4
         side = zh if half == 0 else 1 - zh
-        places = [((y + dy) % 4) * 2 + (core + dc) % 2 for dy, dc in members]
-        ats = [there * GRID + side * 8 + p for p in places]
-        lows = [low_s[at] for at in ats]
+        uppers = [side * 8 + ((y + dy) % 4) * 2 + (core + dc) % 2 for dy, dc in members]
+        lows = [sides[there, upper] for upper in uppers]
         dims = (((1,), (1,)), ((), ()))
         both = [
             lax.dot_general(
@@ -235,13 +234,13 @@
         ]
         both = both[0] + both[1]
         level = occ_s[there * 4 + col // 4]
-        for i, (place, at) in enumerate(zip(places, ats)):
+        for i, upper in enumerate(uppers):
             mine = both[i * BLOCK : (i + 1) * BLOCK]
-            right = side_of[at]
-            across = jnp.where(right > 0.5, second_line, first_line) - level
-            kept = jnp.where(jnp.broadcast_to(right, (BLOCK, BLOCK)) > 0.5, mine[:, BLOCK:], mine[:, :BLOCK])
-            below = gaps[(side * 8 + place) * 2 + lows[i]] + across
-            dense[at] = (kept / below).astype(jnp.bfloat16)
+            right = jnp.full((1, BLOCK), sides[GRID + there, GRID + upper])
+            across = jnp.where(right > 0, second_line, first_line) - level
+            kept = jnp.where(jnp.broadcast_to(right, (BLOCK, BLOCK)) > 0, mine[:, BLOCK:], mine[:, :BLOCK])
+            below = gaps[upper * 2 + lows[i]] + across
+            dense[there * GRID + upper] = (kept / below).astype(jnp.bfloat16)
 
     def compute(group, *todo):
         for first, step, count in todo:
@@ -328,7 +327,7 @@
         send("yf", 1, flow)
     for flow in (0, 1):
         got("x", 2, flow, 1 - flow)
-    compute(0, (9, 2, 2))
+    compute(0, (9, 2, 2), (12, 1, 1))
     for flow in (0, 1):
         got("y", 1, flow, 1 - flow)
     for dy in (1, 3):
@@ -338,9 +337,9 @@
     send_line(2)
     for flow in (0, 1):
         got("xf", 1, flow)
-    compute(0, (6, 6, 2))
+    compute(0, (6, 1, 1))
     half_ready(1, (0, 1, 3))
-    compute(1, (0, 1, 6))
+    compute(1, (0, 1, 10))
     for flow in (0, 1):
         got("x", 3, flow, flow)
         send("xf", 3, flow)
@@ -352,7 +351,7 @@
     for flow in (0, 1):
         got("xf", 2, flow)
     compute(0, (10, 1, 1))
-    compute(1, (6, 1, 7))
+    compute(1, (10, 1, 3))
     half_ready(1, (2,))
     compute(2, (0, 1, 13))
     for flow in (0, 1):
@@ -375,14 +374,14 @@
                 descriptor(("w", flow, dist, piece)).wait_send()
 
 
-def products(low, amplitudes, integrals, side_of, occ_energy, vir_energy):
+def products(sides, amplitudes, integrals, occ_energy, vir_energy):
     anywhere = pl.BlockSpec(memory_space=pl.ANY)
     vmem = pl.BlockSpec(memory_space=pltpu.VMEM)
     pairs = len(KEYS)
     return pl.pallas_call(
         exchange,
         out_shape=pltpu.VMEM((CELLS + 8, BLOCK, BLOCK), jnp.bfloat16),
-        in_specs=[pl.BlockSpec(memory_space=pltpu.SMEM), anywhere, anywhere, vmem, anywhere, anywhere],
+        in_specs=[pl.BlockSpec(memory_space=pltpu.SMEM)] + [anywhere] * 4,
         out_specs=vmem,
         scratch_shapes=[
             pltpu.VMEM((UNITS, 2, 2, BLOCK, DEPTH), jnp.bfloat16),
@@ -400,31 +399,31 @@
             collective_id=0, has_side_effects=True, vmem_limit_bytes=LIMIT
         ),
         name="exchange",
-    )(low, amplitudes, integrals, side_of, occ_energy, vir_energy)
+    )(sides, amplitudes, integrals, occ_energy, vir_energy)
 
 
 def ordered(ranks, dense, out, sem):
     def put(src, slot):
         pltpu.make_async_copy(dense.at[src], out.at[0, 0, slot], sem.at[0]).start()
 
-    def some(t, carry):
-        for i in range(8):
-            at = t * 8 + i
-            rank = ranks[at]
+    def some(t, count):
+        for i in range(GRID):
+            rank = ranks[t, i]
 
             @pl.when(rank > 0)
             def _():
-                put(at, rank - 1)
-
-        return carry
-
-    lax.fori_loop(0, CELLS // 8, some, 0)
+                put(t * GRID + i, rank - 1)
+
+            count = count + jnp.minimum(rank, 1)
+        return count
+
+    count = lax.fori_loop(0, GRID, some, jnp.int32(0))
 
     def rest(slot, carry):
         put(CELLS, slot)
         return carry
 
-    lax.fori_loop(ranks[CELLS], TILES, rest, 0)
+    lax.fori_loop(count, TILES, rest, 0)
     whole = dense.at[pl.ds(0, TILES)]
     pltpu.make_async_copy(whole, out.at[0, 0], sem.at[0]).wait()
 
@@ -444,23 +443,25 @@
 
 def shards(amplitudes, integrals, block_mask, occ_energy, vir_energy):
     col = lax.axis_index("col")
-    cell = lax.dynamic_index_in_dim(block_mask.reshape(32, GRID, GRID, 2), col, 2, keepdims=False)
-    four = cell.reshape(GRID, 2, GRID, 2)
-    low = jnp.sum(four[:, 1], axis=2).T.reshape(CELLS)
-    right = jnp.sum(four[..., 1], axis=1).T
-    side_of = jnp.broadcast_to(right.astype(jnp.float32).reshape(CELLS, 1, 1), (CELLS, 1, BLOCK))
-    flat = cell.reshape(32, 32).astype(jnp.float32)
-    at = jnp.arange(32)
-    inside = flat @ (at[:, None] <= at[None, :]).astype(jnp.float32)
-    ahead = (at[None, :] < at[:, None]).astype(jnp.float32) @ inside[:, 31:]
-    upto = inside + ahead
-    ranks = jnp.sum((flat * upto).reshape(GRID, 2, GRID, 2), axis=(1, 3)).T.reshape(CELLS)
-    ranks = jnp.concatenate([ranks, jnp.broadcast_to(upto[31, 31:], (CELLS,))]).astype(jnp.int32)
+
+    def chosen(shape, test):
+        down, across = (lax.broadcasted_iota(jnp.int32, shape, axis) for axis in (0, 1))
+        return test(down, across).astype(jnp.float32)
+
+    pick = chosen((32, 512), lambda v, at: at == v // 2 * 32 + 2 * col + v % 2)
+    cell = lax.dot_general(pick, block_mask.astype(jnp.float32), (((1,), (1,)), ((), ())))
+    rows = chosen((GRID, 32), lambda r, v: v // 2 == r)
+    lines = chosen((32, GRID), lambda u, c: u // 2 == c)
+    all_rows = chosen((32, 32), lambda r, v: jnp.where(r < GRID, v // 2 == r, v == 2 * (r - GRID) + 1))
+    all_lines = chosen((32, 32), lambda u, c: jnp.where(c < GRID, u == 2 * c + 1, u // 2 == c - GRID))
+    sides = (all_rows @ (cell @ all_lines)).astype(jnp.int32)
+    upto = chosen((32, 32), lambda v, at: at <= v) @ cell
+    upto = upto + jnp.sum(cell, axis=0, keepdims=True) @ chosen((32, 32), lambda at, u: at < u)
+    ranks = (rows @ ((cell * upto) @ lines)).astype(jnp.int32)
     dense = products(
-        low,
+        sides,
         amplitudes.reshape(2, BLOCK, DEPTH),
         integrals.reshape(2, BLOCK, DEPTH),
-        side_of,
         occ_energy,
         vir_energy.reshape(8, BLOCK),
     )

time: 117 us -> 115 us (0.983)
  local copies, waits for them, and re-layouts: 3.9 us -> 0 us
  matrix products: 0.31 us -> 2.57 us
    dot_general x2 -> x5, matrix products: 0.31 us -> 2.57 us  [the longest x1 1.07 us: shards(): lax.dot_general(pick, block_mask.astype(jnp.float32), (((1,), (1,)), ((),...]
where the time goes in v4:
time: 115 us
  Pallas kernels  112 us (97%)
  matrix products  2.57 us (2%)
    pallas_call x1, Pallas kernels, products(): pl.pallas_call(exchange, out_shape=pltpu.VMEM((CELLS + 8, BLOCK, BLOCK),...  108 us
    pallas_call x1, Pallas kernels, in_order(): pl.pallas_call(ordered, out_shape=jax.ShapeDtypeStruct((1, 1, TILES, BLOC...  3.24 us

profile of v4, /device:TPU:1, one launch (start us, length us, event | category | flops | bytes accessed | tf_op | source)
XLA Modules:
  0.0 114.5 jit_solution(11976518980688830419)
XLA Ops:
  0.1 1.1 fusion.52
  1.1 0.1 convolution_bitcast_fusion
  1.3 0.1 fusion.5
  1.4 0.9 convolution_convert_fusion.sides
  2.3 0.3 fusion.6.ranks
  2.6 108.5 %exchange.1.dense = bf16[264,128,128]{2,1,0:T(8,128)(2,1)S(1)} custom-call(s32[32,32]{1,0:T(8,128)} %convolution_convert_fusion.sides, bf16[2,128,768]{2,1,0:T(8,128)(2,1)} %bitcast.11, bf16[2,128,768]{2,1,0:T(8,128)(2,1)} %bitcast.12, f32[64]{0:T(128)} %occ.1, f32[8,128]{1,0:T(8,128)} %bitcast.13), custom_call_target="tpu_custom_call" | custom-call | tf_op jit(solution)/shard_map/exchange/pallas_call | solution.py:381
  111.1 3.2 %ordered.1 = bf16[1,1,192,128,128]{4,3,2,1,0:T(8,128)(2,1)} custom-call(s32[16,16]{1,0:T(8,128)S(1)} %fusion.6.ranks, bf16[264,128,128]{2,1,0:T(8,128)(2,1)S(1)} %exchange.1.dense), custom_call_target="tpu_custom_call" | custom-call | tf_op jit(solution)/shard_map/ordered/pallas_call | solution.py:433
  (6 shorter events, 0.0 us)

commit v5 on v4

--- a/solution.py
+++ b/solution.py
@@ -109,6 +109,8 @@
             return near.at[dy * 2 + dc, piece]
         return last.at[dc, piece] if dy == 2 else far.at[(0, 1, 0, 2)[dy] * 2 + dc, piece]
 
+    early = table(zl, (1, 1, 0, 0))
+
     def line_slot(flow, dist, ahead):
         step = -1 if flow else 1
         slots = []
@@ -137,6 +139,8 @@
             there = at_z(ring_of[flow])
         elif kind == "x":
             _, k, flow, piece = key
+            if k == 2:
+                piece = early if piece == 0 else 1 - early
             src = store.at[slot_k[k], piece]
             dst = store.at[CROSS + (2 if flow == 0 else 0) * 4 + k, piece]
             there = at_x(step_of[flow])
@@ -207,25 +211,27 @@
             send(kind, at, 0, i)
             send(kind, at, 1, 1 - i)
 
-    groups = (
-        (near, 0, [(dy, dc) for dy in range(4) for dc in (0, 1)]),
-        (far, 1, [(dy, dc) for dy in (0, 1, 3) for dc in (0, 1)]),
-        (last, 1, [(2, dc) for dc in (0, 1)]),
+    parts = (
+        [(near, i, 0, i // 2, i % 2) for i in range(8)],
+        [(far, i, 1, (0, 1, 3)[i // 2], i % 2) for i in range(6)],
+        [(last, i, 1, 2, i) for i in range(2)],
     )
+    groups = (*parts, parts[0] + parts[1] + parts[2])
     first_line = vir[pl.ds((2 * col) % 8, 1), :]
     second_line = vir[pl.ds((2 * col + 1) % 8, 1), :]
 
     def chunk(group, k, dx):
-        rows_ref, half, members = groups[group]
+        members = groups[group]
         unit = slot_k[k] if dx == 0 else CROSS + (dx - 1) * 4 + k
         there = line_k[k] * 4 + (x + dx) % 4
-        side = zh if half == 0 else 1 - zh
-        uppers = [side * 8 + ((y + dy) % 4) * 2 + (core + dc) % 2 for dy, dc in members]
+        uppers = [
+            (1 - zh if half else zh) * 8 + ((y + dy) % 4) * 2 + (core + dc) % 2 for _, _, half, dy, dc in members
+        ]
         lows = [sides[there, upper] for upper in uppers]
         dims = (((1,), (1,)), ((), ()))
         both = [
             lax.dot_general(
-                jnp.concatenate([rows_ref[i, piece, low] for i, low in enumerate(lows)], axis=0),
+                jnp.concatenate([ref[i, piece, low] for (ref, i, *_), low in zip(members, lows)], axis=0),
                 store[unit, 1 - piece].reshape(UNIT, DEPTH),
                 dims,
                 preferred_element_type=jnp.float32,
@@ -285,84 +291,85 @@
     for flow in (0, 1):
         got("z", flow, 2, flow)
         send("z", flow, 3, flow)
-        send("z", flow, 2, 1 - flow)
     for flow in (0, 1):
         got("yf", 0, flow)
         send("c", 0, 2, flow)
-    half_ready(0, range(4))
-    compute(0, (0, 1, 1))
     for flow in (0, 1):
         got("z", flow, 3, flow)
         send("z", flow, 4, flow)
+        send("z", flow, 2, 1 - flow)
     for flow in (0, 1):
         got("x", 0, flow, 1 - flow)
         got("x", 1, flow, flow)
         send("xf", 1, flow)
-    compute(0, (1, 2, 2))
-    for flow in (0, 1):
-        got("z", flow, 2, 1 - flow)
-        send("z", flow, 3, 1 - flow)
-    send_unit("x", 2)
-    for flow in (0, 1):
-        got("xf", 0, flow)
-    send_line(1)
-    compute(0, (2, 2, 2))
-    for flow in (0, 1):
-        got("x", 1, flow, 1 - flow)
-    compute(0, (5, 2, 2))
+    for flow in (0, 1):
+        send("x", 2, flow, 0)
     for flow in (0, 1):
         got("z", flow, 4, flow)
     send_unit("y", 1)
     send("c", 1, 0, 0)
     send("c", 1, 0, 1)
-    for flow in (0, 1):
-        got("x", 2, flow, flow)
-        send("xf", 2, flow)
-    compute(0, (8, 1, 1))
+    half_ready(0, range(4))
+    compute(0, (0, 1, 2), (3, 1, 1))
+    for flow in (0, 1):
+        got("xf", 0, flow)
+        got("x", 1, flow, 1 - flow)
+    compute(0, (2, 2, 2))
+    for flow in (0, 1):
+        got("z", flow, 2, 1 - flow)
+        send("z", flow, 3, 1 - flow)
+    for flow in (0, 1):
+        send("x", 2, flow, 1)
+    send_line(1)
+    for flow in (0, 1):
+        got("y", 1, flow, flow)
+        send("yf", 1, flow)
+    compute(0, (5, 2, 2), (8, 1, 1))
     for flow in (0, 1):
         got("z", flow, 3, 1 - flow)
     send_unit("x", 3)
-    for flow in (0, 1):
-        got("y", 1, flow, flow)
-        send("yf", 1, flow)
-    for flow in (0, 1):
-        got("x", 2, flow, 1 - flow)
-    compute(0, (9, 2, 2), (12, 1, 1))
     for flow in (0, 1):
         got("y", 1, flow, 1 - flow)
     for dy in (1, 3):
         send("c", 1, dy, 0)
         send("c", 1, dy, 1)
+    for flow in (0, 1):
+        got("x", 2, flow, 0)
+        got("x", 2, flow, 1)
+    for flow in (0, 1):
+        send("xf", 2, flow)
+    compute(0, (12, 1, 1))
+    half_ready(1, (0, 1, 3))
+    compute(1, (0, 1, 2))
     got_line(1)
     send_line(2)
     for flow in (0, 1):
+        got("yf", 1, flow)
+        send("c", 1, 2, flow)
+    compute(0, (9, 2, 2))
+    compute(1, (2, 1, 4))
+    for flow in (0, 1):
+        got("x", 3, flow, flow)
+        send("xf", 3, flow)
+    compute(1, (7, 1, 2))
+    got_line(2)
+    send_line(3)
+    for flow in (0, 1):
         got("xf", 1, flow)
     compute(0, (6, 1, 1))
-    half_ready(1, (0, 1, 3))
-    compute(1, (0, 1, 10))
-    for flow in (0, 1):
-        got("x", 3, flow, flow)
-        send("xf", 3, flow)
-    for flow in (0, 1):
-        got("yf", 1, flow)
-        send("c", 1, 2, flow)
-    got_line(2)
-    send_line(3)
+    compute(1, (6, 1, 1), (9, 2, 2), (12, 1, 1))
+    half_ready(1, (2,))
+    compute(2, (0, 1, 10), (11, 1, 2))
     for flow in (0, 1):
         got("xf", 2, flow)
-    compute(0, (10, 1, 1))
-    compute(1, (10, 1, 3))
-    half_ready(1, (2,))
-    compute(2, (0, 1, 13))
+    compute(3, (10, 1, 1))
     for flow in (0, 1):
         got("x", 3, flow, 1 - flow)
-    for group in range(3):
-        compute(group, (13, 2, 2))
+    compute(3, (13, 2, 2))
     for flow in (0, 1):
         got("xf", 3, flow)
     got_line(3)
-    for group in range(3):
-        compute(group, (14, 2, 1))
+    compute(3, (14, 1, 1))
 
     for copy in started:
         copy.wait_send()

time: 115 us -> 118 us (1.026)
  Pallas kernels: 112 us -> 115 us
    pallas_call x1, Pallas kernels: 108 us -> 112 us  [products(): pl.pallas_call(exchange, out_shape=pltpu.VMEM((CELLS + 8, BLOCK, BLOCK),...]
where the time goes in v5:
time: 118 us
  Pallas kernels  115 us (97%)
  matrix products  2.57 us (2%)
    pallas_call x1, Pallas kernels, products(): pl.pallas_call(exchange, out_shape=pltpu.VMEM((CELLS + 8, BLOCK, BLOCK),...  112 us
    pallas_call x1, Pallas kernels, in_order(): pl.pallas_call(ordered, out_shape=jax.ShapeDtypeStruct((1, 1, TILES, BLOC...  3.24 us

profile of v5, /device:TPU:1, one launch (start us, length us, event | category | flops | bytes accessed | tf_op | source)
XLA Modules:
  0.0 118.0 jit_solution(6529350273412934789)
XLA Ops:
  0.1 1.1 fusion.52
  1.1 0.1 convolution_bitcast_fusion
  1.3 0.1 fusion.5
  1.4 0.9 convolution_convert_fusion.sides
  2.3 0.3 fusion.6.ranks
  2.6 112.0 %exchange.1.dense = bf16[264,128,128]{2,1,0:T(8,128)(2,1)S(1)} custom-call(s32[32,32]{1,0:T(8,128)} %convolution_convert_fusion.sides, bf16[2,128,768]{2,1,0:T(8,128)(2,1)} %bitcast.11, bf16[2,128,768]{2,1,0:T(8,128)(2,1)} %bitcast.12, f32[64]{0:T(128)} %occ.1, f32[8,128]{1,0:T(8,128)} %bitcast.13), custom_call_target="tpu_custom_call" | custom-call | tf_op jit(solution)/shard_map/exchange/pallas_call | solution.py:388
  114.6 3.2 %ordered.1 = bf16[1,1,192,128,128]{4,3,2,1,0:T(8,128)(2,1)} custom-call(s32[16,16]{1,0:T(8,128)S(1)} %fusion.6.ranks, bf16[264,128,128]{2,1,0:T(8,128)(2,1)S(1)} %exchange.1.dense), custom_call_target="tpu_custom_call" | custom-call | tf_op jit(solution)/shard_map/ordered/pallas_call | solution.py:440
  (6 shorter events, 0.0 us)
